TPU v7x, 256 devices: a whole 4x4x8 slice. The times are simulated.
256 devices in a mesh: segment: 2 (over x_lo), seq: 16 (over y, x_hi, core), mp: 8 (over z).
Axes of the slice: x: 4 (x_hi: 2, x_lo: 2; x = x_hi * 2 + x_lo), y: 4, z: 8, core: 2. Of those that a mesh axis runs over, the one named last changes fastest.
Arguments:
- enc_states: bfloat16 [4096, 4096], P('seq', 'mp'), may hold values from -6 to 6
- dec_states: bfloat16 [4096, 4096], P('seq', 'mp'), may hold values from -21 to 21
- section_weights: bfloat16 [2, 4096, 2, 4096], P('segment', None, None, 'mp'), may hold values from -3 to 3
- group_lengths: int32 [32], P('seq'), may hold values from 1 to 128, 3072 in all
Outputs:
- mixed: bfloat16 [4096, 4096], P('seq', ('segment', 'mp'))
Inputs may be any that keep to these rules, and one draw needn't show every extreme that they name: Rows c * 128 to c * 128 + group_lengths[c] - 1 of the memory are real, the rest of block c is padding.
All inputs are finite; a program needn't handle non-finite values.
Results may differ from a plain program's by a relative error of at most 0.018.
Values may be sent and summed in bfloat16 or wider, within the bound.
A program may use at most 128 MiB of HBM per device.

v0:
```python
import math
import jax
import jax.numpy as jnp
from jax import lax
from jax.sharding import PartitionSpec as P

DH = 256
GROUP = 128


def from_behind(value, axis, steps):
    count = lax.axis_size(axis)
    leading, last = (max(0, -steps), min(count, count - steps))
    return lax.ppermute(value, axis, [(source, source + steps) for source in range(leading, last)])


def local(enc_states, dec_states, section_weights, group_lengths):
    encoder_side = lax.axis_index("segment") == 0
    local_weight = section_weights[0]
    width = local_weight.shape[0]
    columns = local_weight.shape[2]
    enc_rows = enc_states.shape[0]
    dec_rows = dec_states.shape[0]
    heads = columns // DH
    scale = DH ** (-0.5)
    start_sums = (
        jnp.zeros((enc_rows, 2 * columns), jnp.float32),
        jnp.zeros((dec_rows, columns), jnp.float32),
    )
    pieces = (
        lax.all_gather(enc_states, "mp", axis=1, tiled=True),
        lax.all_gather(dec_states, "mp", axis=1, tiled=True),
    )
    rows_in = pieces[0].shape[1]

    def encoder_work(state):
        update = jnp.dot(
            pieces[0],
            local_weight.reshape(rows_in, 2 * columns),
            preferred_element_type=jnp.float32,
        )
        return (update, state[1])

    def decoder_work(state):
        update = jnp.dot(pieces[1], local_weight[:, 0, :], preferred_element_type=jnp.float32)
        return (state[0], update)

    memory_sum, query_sum = lax.cond(encoder_side, encoder_work, decoder_work, start_sums)
    memory = memory_sum.astype(jnp.bfloat16)
    queries = query_sum.astype(jnp.bfloat16).reshape(dec_rows, heads, DH)
    received = from_behind(memory, "segment", 1)
    start_state = (
        jnp.full((dec_rows, heads), -1e30, jnp.float32),
        jnp.zeros((dec_rows, heads), jnp.float32),
        jnp.zeros((dec_rows, heads, DH), jnp.float32),
    )
    carry = start_state
    memory_piece = lax.all_gather(received, "seq", axis=0, tiled=True)
    length_piece = lax.all_gather(group_lengths, "seq", axis=0, tiled=True)
    amount = memory_piece.shape[0]
    span = math.gcd(amount, 1024)
    block_total = amount // span
    memory_blocks = memory_piece.reshape(block_total, span, 2 * columns)
    length_blocks = length_piece.reshape(block_total, span // GROUP)

    def one_block(state, item):
        best, total, accum = state
        block, lengths = item
        block_keys = block[:, :columns].reshape(span, heads, DH)
        block_values = block[:, columns:].reshape(span, heads, DH)
        scores = (
            jnp.einsum("qhd,khd->qhk", queries, block_keys, preferred_element_type=jnp.float32)
            * scale
        )
        valid = (jnp.arange(GROUP)[None, :] < lengths[:, None]).reshape(span)
        scores = jnp.where(valid[None, None, :], scores, -1e30)
        new_best = jnp.maximum(best, jnp.max(scores, axis=2))
        shrink = jnp.exp(best - new_best)
        weights = jnp.exp(scores - new_best[:, :, None]).astype(jnp.bfloat16)
        total = total * shrink + jnp.sum(weights, axis=2, dtype=jnp.float32)
        accum = accum * shrink[:, :, None] + jnp.einsum(
            "qhk,khd->qhd", weights, block_values, preferred_element_type=jnp.float32
        )
        return ((new_best, total, accum), None)

    carry, _ = lax.scan(one_block, carry, (memory_blocks, length_blocks))
    best, total, accum = carry
    attended = (accum / total[:, :, None]).astype(jnp.bfloat16).reshape(dec_rows, columns)

    def no_term(operand):
        return jnp.zeros((dec_rows, width), jnp.float32)

    def output_term(operand):
        projected = lax.dot_general(
            operand,
            local_weight[:, 1, :],
            (((1,), (1,)), ((), ())),
            preferred_element_type=jnp.float32,
        )
        offset = lax.axis_index("mp") * columns
        current = lax.dynamic_slice_in_dim(projected, offset, columns, 1)
        return lax.dynamic_update_slice_in_dim(
            projected, current + dec_states.astype(jnp.float32), offset, 1
        )

    term = lax.cond(encoder_side, no_term, output_term, attended)
    return lax.psum_scatter(
        term.astype(jnp.bfloat16), ("segment", "mp"), scatter_dimension=1, tiled=True
    )


def solution(mesh):
    in_specs = (P("seq", "mp"), P("seq", "mp"), P("segment", None, None, "mp"), P("seq"))
    out_specs = P("seq", ("segment", "mp"))
    return jax.shard_map(local, mesh=mesh, in_specs=in_specs, out_specs=out_specs, check_vma=False)
```

profile of v0, /device:TPU:8, one launch (start us, length us, event | category | flops | bytes accessed | tf_op | source)
XLA Modules:
  0.0 328.2 jit_solution(9274638926449847188)
XLA Ops:
  6.5 0.7 all-gather.6.cloned.1.call-update
  7.3 0.7 all-gather.4.cloned.1.call-update
  8.1 8.0 %copy.20 = bf16[1,4096,2,512]{3,1,2,0:T(8,128)(2,1)} copy(bf16[1,4096,2,512]{3,2,1,0:T(2,128)(2,1)} %param.12) | data formatting | bytes 16777216 | tf_op args[2]
  16.0 37.2 %all-gather.6.cloned.1.call-done = bf16[256,4096]{1,0:T(8,128)(2,1)} async-done(((bf16[256,512]{1,0:T(8,128)(2,1)}), bf16[256,4096]{1,0:T(8,128)(2,1)}) %all-gather.6.cloned.1.call-update) | async-done | bytes 2097168 | tf_op jit(solution)/shard_map/all_gather | solution.py:31
  53.2 41.5 %all-gather.4.cloned.1.call-done = bf16[256,4096]{1,0:T(8,128)(2,1)} async-done(((bf16[256,512]{1,0:T(8,128)(2,1)}), bf16[256,4096]{1,0:T(8,128)(2,1)}) %all-gather.4.cloned.1.call-update) | async-done | bytes 2097168 | tf_op jit(solution)/shard_map/all_gather | solution.py:32
  94.7 15.2 %conditional.2 = (bf16[256,1024]{1,0:T(8,128)(2,1)S(1)}, bf16[256,512]{1,0:T(8,128)(2,1)S(1)}) conditional(s32[]{:T(128)} %convert_element_type.25, (bf16[4096,2,512]{2,0,1:T(8,128)(2,1)}, bf16[256,4096]{1,0:T(8,128)(2,1)}) %tuple.67, (bf16[1,4096,2,512]{3,2,1,0:T(2,128)(2,1)}, bf16[256,4096]{1,0:T(8,128)(2,1)}) %tuple.24), branch_computations={%region_0.0_spmd, %region_1.0_spmd} | conditional | flops 2147483648 | bytes 36438064 | solution.py:48
  94.7 9.5 %copy.18 = bf16[512,8,2,512]{3,1,2,0:T(8,128)(2,1)} copy(bf16[512,8,2,512]{3,2,1,0:T(2,128)(2,1)} %bitcast.70) | data formatting | bytes 16777216 | tf_op jit(solution)/shard_map/cond
  104.2 5.7 %fusion.14 = bf16[256,1024]{1,0:T(8,128)(2,1)S(1)} fusion(bf16[256,4096]{1,0:T(8,128)(2,1)S(1)} %copy-done.4, bf16[4096,1024]{1,0:T(8,128)(2,1)} %bitcast.75), kind=kOutput, calls=%fused_computation.28 | convolution fusion | flops 2147483648 | bytes 11010048 | tf_op jit(solution)/shard_map/cond/branch_1_fun/dot_general | solution.py:37
  109.9 1.3 collective-permute-start
  111.2 7.7 %collective-permute-done = bf16[256,1024]{1,0:T(8,128)(2,1)S(1)} collective-permute-done((bf16[256,1024]{1,0:T(8,128)(2,1)S(1)}, bf16[256,1024]{1,0:T(8,128)(2,1)S(1)}, u32[]{:S(2)}, u32[]{:S(2)}) %collective-permute-start) | collective-permute-done | bytes 524320 | tf_op jit(solution)/shard_map/ppermute | solution.py:14
  119.0 0.8 copy-done.3
  119.9 0.6 dynamic-slice
  121.4 12.5 %all-reduce = s32[32]{0:T(128)S(1)} all-reduce(s32[32]{0:T(128)S(1)} %dynamic-update-slice), channel_id=1, replica_groups=mesh['segment'=2,'seq'=16,'mp'=8] {'seq'}, use_global_device_ids=true, to_apply=%add | all-reduce | flops 32 | bytes 256
  134.3 61.9 %all-gather.8.cloned.1.call-done = bf16[4096,1024]{1,0:T(8,128)(2,1)} async-done(((bf16[256,1024]{1,0:T(8,128)(2,1)}), bf16[4096,1024]{1,0:T(8,128)(2,1)}) %all-gather.8.cloned.1.call-update) | async-done | bytes 8388624 | tf_op jit(solution)/shard_map/all_gather | solution.py:58
  196.2 39.4 %while.15 = (s32[]{:T(128)}, f32[256,2]{0,1:T(2,128)S(1)}, f32[256,2]{0,1:T(2,128)S(1)}, f32[256,2,256]{0,2,1:T(8,128)}, s32[4,8]{1,0:T(4,128)S(1)}, /*index=5*/...) while((s32[]{:T(128)}, f32[256,2]{0,1:T(2,128)S(1)}, ...), condition=%wide.region_5.6_spmd.clone, body=%wide.region_2.5_spmd.clone.sunk | while | flops 544083456 | bytes 26513672 | solution.py:86
  196.3 3.1 constant_dynamic-slice_fusion.2
  199.4 2.9 copy.22
  202.5 1.0 bitcast_reduce_fusion.2
  203.5 0.5 convert_reduce_fusion.2
  204.0 0.5 copy-done.1
  204.5 0.7 fusion.39
  205.3 0.8 copy-done.2
  206.2 3.1 constant_dynamic-slice_fusion.2
  209.3 2.9 copy.22
  212.3 1.0 bitcast_reduce_fusion.2
  213.4 0.5 convert_reduce_fusion.2
  213.9 0.5 copy-done.1
  214.4 0.7 fusion.39
  215.1 0.8 copy-done.2
  216.0 3.1 constant_dynamic-slice_fusion.2
  219.1 2.9 copy.22
  222.2 1.0 bitcast_reduce_fusion.2
  223.2 0.5 convert_reduce_fusion.2
  223.7 0.5 copy-done.1
  224.2 0.7 fusion.39
  225.0 0.8 copy-done.2
  225.9 3.1 constant_dynamic-slice_fusion.2
  229.0 2.9 copy.22
  232.0 1.0 bitcast_reduce_fusion.2
  233.1 0.5 convert_reduce_fusion.2
  233.6 0.5 copy-done.1
  234.1 0.7 fusion.39
  234.8 0.8 copy-done.2
  235.7 1.1 divide_convert_fusion
  236.7 2.5 conditional.3
  236.8 2.5 broadcast.17
  239.2 3.8 %convert_element_type.29 = bf16[256,4096]{1,0:T(8,128)(2,1)} convert(f32[256,4096]{1,0:T(8,128)} %get-tuple-element.217) | non-fusion elementwise | flops 1048576 | bytes 6291456 | tf_op jit(solution)/shard_map/convert_element_type | solution.py:108
  243.1 78.6 %reduce-scatter.2.cloned.1.call-done = bf16[256,256]{1,0:T(8,128)(2,1)} async-done(((bf16[256,4096]{1,0:T(8,128)(2,1)}), bf16[256,256]{1,0:T(8,128)(2,1)}) %reduce-scatter.2.cloned.1.call-update) | async-done | bytes 131088 | tf_op jit(solution)/shard_map/reduce_scatter | solution.py:107
  (54 shorter events, 1.9 us)
Async XLA Ops:
  6.5 46.6 %all-gather.6.cloned.1.call-start = ((), (), s32[]{:S(2)}) async-start(), calls=%async_computation.2 | async-start | bytes 2359296 | tf_op jit(solution)/shard_map/all_gather | solution.py:31
  7.3 87.4 %all-gather.4.cloned.1.call-start = ((), (), s32[]{:S(2)}) async-start(), calls=%async_computation.1 | async-start | bytes 2359296 | tf_op jit(solution)/shard_map/all_gather | solution.py:32
  8.0 188.2 %all-gather.8.cloned.1.call-start = ((), (), s32[]{:S(2)}) async-start(), calls=%async_computation.3 | async-start | bytes 8912896 | tf_op jit(solution)/shard_map/all_gather | solution.py:58
  94.7 25.2 %copy-start.6 = (u32[256]{0:T(256)S(1)}, u32[256]{0:T(256)}, u32[]{:S(2)}) copy-start(u32[256]{0:T(256)} %constant.50) | copy-start | bytes 3076
  94.7 26.5 %copy-start.5 = (s32[2]{0:T(128)S(1)}, s32[2]{0:T(128)}, u32[]{:S(2)}) copy-start(s32[2]{0:T(128)} %param.13) | copy-start | bytes 28
  94.7 9.5 %copy-start.4 = (bf16[256,4096]{1,0:T(8,128)(2,1)S(1)}, bf16[256,4096]{1,0:T(8,128)(2,1)}, u32[]{:S(2)}) copy-start(bf16[256,4096]{1,0:T(8,128)(2,1)} %get-tuple-element.53) | copy-start | bytes 6291460 | tf_op jit(solution)/shard_map/cond
  109.9 9.1 %collective-permute-start = (bf16[256,1024]{1,0:T(8,128)(2,1)S(1)}, bf16[256,1024]{1,0:T(8,128)(2,1)S(1)}, u32[]{:S(2)}, u32[]{:S(2)}) collective-permute-start(bf16[256,1024]{1,0:T(8,128)(2,1)S(1)} %get-tuple-element.70), channel_id=1, source_target_pairs={{0,128},{1,129},{2,130},{3,131},{4,132},{5,133},{6,134},{7,135},{8... | collective-permute-start | bytes 1572872 | tf_op jit(solution)/shard_map/ppermute | solution.py:14
  119.0 0.8 copy-start.3
  119.8 201.9 %reduce-scatter.2.cloned.1.call-start = ((), (), s32[]{:S(2)}) async-start(), calls=%async_computation.4 | async-start | bytes 2228224 | tf_op jit(solution)/shard_map/reduce_scatter | solution.py:107
  203.5 1.0 copy-start.1
  205.3 0.8 copy-start.2
  213.3 1.0 copy-start.1
  215.1 0.8 copy-start.2
  223.2 1.0 copy-start.1
  225.0 0.8 copy-start.2
  233.0 1.0 copy-start.1
  234.8 0.8 copy-start.2
Sparse Core Ops, SparseCore 0:
  9.1 43.9 all-gather.5
  55.0 39.6 all-gather.3
  119.9 76.2 all-gather.7
  243.2 78.4 reduce-scatter.1
where the time goes:
time: 329 us; the launch traced here: 328 us
  waiting for transfers between devices  228 us (69%)
  local copies, waits for them, and re-layouts  51.7 us (16%)
  between operations  13.9 us (4%)
  matrix products  12.7 us (4%)
  blocking collectives  12.5 us (4%)
  other arithmetic  7.33 us (2%)
    reduce_scatter x1, waiting for transfers between devices, local(): lax.psum_scatter(term.astype(jnp.bfloat16), ('segment', 'mp'), scatter_di...  78.6 us
    all_gather x1, waiting for transfers between devices, local(): memory_piece = lax.all_gather(received, 'seq', axis=0, tiled=True)  61.9 us
    all_gather x1, waiting for transfers between devices, local(): lax.all_gather(dec_states, 'mp', axis=1, tiled=True)  41.5 us
    all_gather x1, waiting for transfers between devices, local(): lax.all_gather(enc_states, 'mp', axis=1, tiled=True)  37.2 us
    dynamic_slice x8, local copies, waits for them, and re-layouts, local(): carry, _ = lax.scan(one_block, carry, (memory_blocks, length_blocks))  23.8 us
    unnamed x1, blocking collectives  12.5 us
    unnamed x11, local copies, waits for them, and re-layouts  9.78 us
    cond x3, local copies, waits for them, and re-layouts  9.49 us
  transfers between devices with their start and end apart: 5, of which 5 were waited for; matrix products, arithmetic and copies ran while one was open for 3% of the time, Pallas kernels for 0%

commit v1 on v0

--- a/solution.py
+++ b/solution.py
@@ -55,7 +55,10 @@
         jnp.zeros((dec_rows, heads, DH), jnp.float32),
     )
     carry = start_state
-    memory_piece = lax.all_gather(received, "seq", axis=0, tiled=True)
+    memory_piece = jnp.concatenate(
+        lax.all_to_all(jnp.stack([received for _ in range(lax.axis_size("seq"))], 0), "seq", 0, 0),
+        axis=0,
+    )
     length_piece = lax.all_gather(group_lengths, "seq", axis=0, tiled=True)
     amount = memory_piece.shape[0]
     span = math.gcd(amount, 1024)

time: 329 us -> 362 us (1.10)
  blocking collectives: 12.5 us -> 99.5 us
  waiting for transfers between devices: 228 us -> 164 us
  starting transfers between devices: 1.44 us -> 8.79 us
    unnamed x1, blocking collectives: 12.5 us -> 99.5 us
    all_gather x1 -> x0, waiting for transfers between devices: 61.9 us -> none  [local(): memory_piece = lax.all_gather(received, 'seq', axis=0, tiled=True)]
    all_to_all x0 -> x1, starting transfers between devices: none -> 7.39 us  [local(): lax.all_to_all(jnp.stack([received for _ in range(lax.axis_size('seq'))],...]
    another operation x1 -> x2, local copies, waits for them, and re-layouts: 2.46 us -> 6.77 us  [the longest x1 4.32 us: local(): jnp.stack([received for _ in range(lax.axis_size('seq'))], 0)]
    unnamed x11 -> x9, local copies, waits for them, and re-layouts: 9.78 us -> 8.91 us
  transfers between devices with their start and end apart: 5 -> 5, of which waited for: 5 -> 4; matrix products, arithmetic and copies ran while one was open for 3% -> 3% of each run, Pallas kernels for 0% -> 0%
where the time goes in v1:
time: 362 us; the launch traced here: 361 us
  waiting for transfers between devices  164 us (45%)
  blocking collectives  99.5 us (27%)
  local copies, waits for them, and re-layouts  55.2 us (15%)
  between operations  13.8 us (4%)
  matrix products  12.7 us (4%)
  starting transfers between devices  8.79 us (2%)
  other arithmetic  7.31 us (2%)
    unnamed x1, blocking collectives  99.5 us
    reduce_scatter x1, waiting for transfers between devices, local(): lax.psum_scatter(term.astype(jnp.bfloat16), ('segment', 'mp'), scatter_di...  76 us
    all_gather x1, waiting for transfers between devices, local(): lax.all_gather(dec_states, 'mp', axis=1, tiled=True)  41.5 us
    all_gather x1, waiting for transfers between devices, local(): lax.all_gather(enc_states, 'mp', axis=1, tiled=True)  37.2 us
    dynamic_slice x8, local copies, waits for them, and re-layouts, local(): carry, _ = lax.scan(one_block, carry, (memory_blocks, length_blocks))  23.8 us
    cond x3, local copies, waits for them, and re-layouts  9.48 us
    unnamed x9, local copies, waits for them, and re-layouts  8.91 us
    ppermute x1, waiting for transfers between devices, from_behind(): lax.ppermute(value, axis, [(source, source + steps) for source in range(l...  7.72 us
  transfers between devices with their start and end apart: 5, of which 4 were waited for; matrix products, arithmetic and copies ran while one was open for 3% of the time, Pallas kernels for 0%

profile of v1, /device:TPU:8, one launch (start us, length us, event | category | flops | bytes accessed | tf_op | source)
XLA Modules:
  0.0 361.4 jit_solution(13337056072990007314)
XLA Ops:
  6.5 0.7 all-gather.5.cloned.1.call-update
  7.3 0.7 all-gather.3.cloned.1.call-update
  8.0 7.9 %copy.20 = bf16[1,4096,2,512]{3,1,2,0:T(8,128)(2,1)} copy(bf16[1,4096,2,512]{3,2,1,0:T(2,128)(2,1)} %param.12) | data formatting | bytes 16777216 | tf_op args[2]
  16.0 37.2 %all-gather.5.cloned.1.call-done = bf16[256,4096]{1,0:T(8,128)(2,1)} async-done(((bf16[256,512]{1,0:T(8,128)(2,1)}), bf16[256,4096]{1,0:T(8,128)(2,1)}) %all-gather.5.cloned.1.call-update) | async-done | bytes 2097168 | tf_op jit(solution)/shard_map/all_gather | solution.py:31
  53.2 41.5 %all-gather.3.cloned.1.call-done = bf16[256,4096]{1,0:T(8,128)(2,1)} async-done(((bf16[256,512]{1,0:T(8,128)(2,1)}), bf16[256,4096]{1,0:T(8,128)(2,1)}) %all-gather.3.cloned.1.call-update) | async-done | bytes 2097168 | tf_op jit(solution)/shard_map/all_gather | solution.py:32
  94.7 15.2 %conditional.2 = (bf16[256,1024]{1,0:T(8,128)(2,1)S(1)}, bf16[256,512]{1,0:T(8,128)(2,1)S(1)}) conditional(s32[]{:T(128)} %convert_element_type.25, (bf16[4096,2,512]{2,0,1:T(8,128)(2,1)}, bf16[256,4096]{1,0:T(8,128)(2,1)}) %tuple.65, (bf16[1,4096,2,512]{3,2,1,0:T(2,128)(2,1)}, bf16[256,4096]{1,0:T(8,128)(2,1)}) %tuple.24), branch_computations={%region_0.0_spmd, %region_1.0_spmd} | conditional | flops 2147483648 | bytes 36438064 | solution.py:48
  94.7 9.5 %copy.18 = bf16[512,8,2,512]{3,1,2,0:T(8,128)(2,1)} copy(bf16[512,8,2,512]{3,2,1,0:T(2,128)(2,1)} %bitcast.70) | data formatting | bytes 16777216 | tf_op jit(solution)/shard_map/cond
  104.2 5.7 %fusion.14 = bf16[256,1024]{1,0:T(8,128)(2,1)S(1)} fusion(bf16[256,4096]{1,0:T(8,128)(2,1)S(1)} %copy-done.3, bf16[4096,1024]{1,0:T(8,128)(2,1)} %bitcast.74), kind=kOutput, calls=%fused_computation.28 | convolution fusion | flops 2147483648 | bytes 11010048 | tf_op jit(solution)/shard_map/cond/branch_1_fun/dot_general | solution.py:37
  109.9 1.3 collective-permute-start
  111.2 7.7 %collective-permute-done = bf16[256,1024]{1,0:T(8,128)(2,1)S(1)} collective-permute-done((bf16[256,1024]{1,0:T(8,128)(2,1)S(1)}, bf16[256,1024]{1,0:T(8,128)(2,1)S(1)}, u32[]{:S(2)}, u32[]{:S(2)}) %collective-permute-start) | collective-permute-done | bytes 524320 | tf_op jit(solution)/shard_map/ppermute | solution.py:14
  119.0 4.3 %stack.2 = bf16[16,256,1024]{2,1,0:T(8,128)(2,1)} broadcast(bf16[256,1024]{1,0:T(8,128)(2,1)S(1)} %collective-permute-done), dimensions={1,2} | broadcast | bytes 8912896 | tf_op jit(solution)/shard_map/stack | solution.py:59
  123.3 7.4 %all-to-all-start = ((bf16[16,256,1024]{2,1,0:T(8,128)(2,1)}), bf16[16,256,1024]{2,1,0:T(8,128)(2,1)}, u32[]{:S(2)}, u32[]{:S(2)}) async-start(bf16[16,256,1024]{2,1,0:T(8,128)(2,1)} %stack.2), calls=%async_computation | async-start | bytes 16777216 | tf_op jit(solution)/shard_map/all_to_all | solution.py:59
  130.8 0.6 dynamic-slice
  132.2 99.5 %all-reduce = s32[32]{0:T(128)S(1)} all-reduce(s32[32]{0:T(128)S(1)} %dynamic-update-slice), channel_id=1, replica_groups=mesh['segment'=2,'seq'=16,'mp'=8] {'seq'}, use_global_device_ids=true, to_apply=%add | all-reduce | flops 32 | bytes 256
  232.1 39.5 %while.15 = (s32[]{:T(128)}, f32[256,2]{0,1:T(2,128)S(1)}, f32[256,2]{0,1:T(2,128)S(1)}, f32[256,2,256]{0,2,1:T(8,128)}, s32[4,8]{1,0:T(4,128)S(1)}, /*index=5*/...) while((s32[]{:T(128)}, f32[256,2]{0,1:T(2,128)S(1)}, ...), condition=%wide.region_5.6_spmd.clone, body=%wide.region_2.5_spmd.clone.sunk | while | flops 544083456 | bytes 26513672 | solution.py:89
  232.2 3.1 constant_dynamic-slice_fusion.2
  235.3 2.9 copy.22
  238.3 1.0 bitcast_reduce_fusion.2
  239.4 0.5 convert_reduce_fusion.2
  239.9 0.5 copy-done.1
  240.4 0.7 fusion.39
  241.1 0.8 copy-done.2
  242.1 3.1 constant_dynamic-slice_fusion.2
  245.1 2.9 copy.22
  248.2 1.0 bitcast_reduce_fusion.2
  249.2 0.5 convert_reduce_fusion.2
  249.8 0.5 copy-done.1
  250.2 0.7 fusion.39
  251.0 0.8 copy-done.2
  251.9 3.1 constant_dynamic-slice_fusion.2
  255.0 2.9 copy.22
  258.1 1.0 bitcast_reduce_fusion.2
  259.1 0.5 convert_reduce_fusion.2
  259.6 0.5 copy-done.1
  260.1 0.7 fusion.39
  260.9 0.8 copy-done.2
  261.8 3.1 constant_dynamic-slice_fusion.2
  264.9 2.9 copy.22
  267.9 1.0 bitcast_reduce_fusion.2
  269.0 0.5 convert_reduce_fusion.2
  269.5 0.5 copy-done.1
  270.0 0.7 fusion.39
  270.7 0.8 copy-done.2
  271.6 1.1 divide_convert_fusion
  272.6 2.5 conditional.3
  272.7 2.5 broadcast.19
  275.1 3.8 %convert_element_type.29 = bf16[256,4096]{1,0:T(8,128)(2,1)} convert(f32[256,4096]{1,0:T(8,128)} %get-tuple-element.217) | non-fusion elementwise | flops 1048576 | bytes 6291456 | tf_op jit(solution)/shard_map/convert_element_type | solution.py:111
  278.9 76.0 %reduce-scatter.2.cloned.1.call-done = bf16[256,256]{1,0:T(8,128)(2,1)} async-done(((bf16[256,4096]{1,0:T(8,128)(2,1)}), bf16[256,256]{1,0:T(8,128)(2,1)}) %reduce-scatter.2.cloned.1.call-update) | async-done | bytes 131088 | tf_op jit(solution)/shard_map/reduce_scatter | solution.py:110
  (52 shorter events, 1.9 us)
Async XLA Ops:
  6.5 46.6 %all-gather.5.cloned.1.call-start = ((), (), s32[]{:S(2)}) async-start(), calls=%async_computation.3 | async-start | bytes 2359296 | tf_op jit(solution)/shard_map/all_gather | solution.py:31
  7.3 87.4 %all-gather.3.cloned.1.call-start = ((), (), s32[]{:S(2)}) async-start(), calls=%async_computation.2 | async-start | bytes 2359296 | tf_op jit(solution)/shard_map/all_gather | solution.py:32
  94.7 9.5 %copy-start.3 = (bf16[256,4096]{1,0:T(8,128)(2,1)S(1)}, bf16[256,4096]{1,0:T(8,128)(2,1)}, u32[]{:S(2)}) copy-start(bf16[256,4096]{1,0:T(8,128)(2,1)} %get-tuple-element.53) | copy-start | bytes 6291460 | tf_op jit(solution)/shard_map/cond
  109.9 9.1 %collective-permute-start = (bf16[256,1024]{1,0:T(8,128)(2,1)S(1)}, bf16[256,1024]{1,0:T(8,128)(2,1)S(1)}, u32[]{:S(2)}, u32[]{:S(2)}) collective-permute-start(bf16[256,1024]{1,0:T(8,128)(2,1)S(1)} %get-tuple-element.70), channel_id=1, source_target_pairs={{0,128},{1,129},{2,130},{3,131},{4,132},{5,133},{6,134},{7,135},{8... | collective-permute-start | bytes 1572872 | tf_op jit(solution)/shard_map/ppermute | solution.py:14
  123.3 7.5 %copy-start.5 = (u32[256]{0:T(256)S(1)}, u32[256]{0:T(256)}, u32[]{:S(2)}) copy-start(u32[256]{0:T(256)} %constant.50) | copy-start | bytes 3076
  123.3 8.7 %copy-start.4 = (s32[2]{0:T(128)S(1)}, s32[2]{0:T(128)}, u32[]{:S(2)}) copy-start(s32[2]{0:T(128)} %param.13) | copy-start | bytes 28
  123.3 108.8 %all-to-all-start = ((bf16[16,256,1024]{2,1,0:T(8,128)(2,1)}), bf16[16,256,1024]{2,1,0:T(8,128)(2,1)}, u32[]{:S(2)}, u32[]{:S(2)}) async-start(bf16[16,256,1024]{2,1,0:T(8,128)(2,1)} %stack.2), calls=%async_computation | async-start | bytes 16777216 | tf_op jit(solution)/shard_map/all_to_all | solution.py:59
  130.7 224.2 %reduce-scatter.2.cloned.1.call-start = ((), (), s32[]{:S(2)}) async-start(), calls=%async_computation.4 | async-start | bytes 2228224 | tf_op jit(solution)/shard_map/reduce_scatter | solution.py:110
  239.3 1.0 copy-start.1
  241.1 0.8 copy-start.2
  249.2 1.0 copy-start.1
  251.0 0.8 copy-start.2
  259.1 1.0 copy-start.1
  260.9 0.8 copy-start.2
  268.9 1.0 copy-start.1
  270.7 0.8 copy-start.2
Sparse Core Ops, SparseCore 0:
  9.1 43.9 all-gather.4
  55.0 39.6 all-gather.2
  279.1 75.8 reduce-scatter.1
